TPU v7x, 32 devices: a whole 2x2x4 slice. The times are simulated.
32 devices in a mesh: dp: 16 (over z, x, core), section: 2 (over y).
Axes of the slice: x: 2, y: 2, z: 4, core: 2. Of those that a mesh axis runs over, the one named last changes fastest.
Arguments:
- section_inputs: bfloat16 [2, 128, 8, 4, 4, 768], P('section', 'dp'), may hold values from -6 to 6
- cotangent: bfloat16 [128, 8, 4, 4, 128], P('dp'), may hold values from -6 to 6
- sessions: int32 [128], P('dp'), may hold values from 0 to 3
- point_weight: bfloat16 [2, 768, 768], P('section', 'dp'), may hold values from -0.21875 to 0.21875
- spatial_kernel: float32 [2, 9, 768], P('section'), may hold values from -1.5 to 1.5
- temporal_kernel: float32 [2, 5, 768], P('section'), may hold values from -2 to 2
- readout: bfloat16 [4, 128, 768], replicated, may hold values from -0.5 to 0.5
Outputs:
- point_grads: float32 [2, 768, 768], P('section', 'dp')
- spatial_grads: float32 [2, 9, 768], P('section')
- temporal_grads: float32 [2, 5, 768], P('section')
All inputs are finite; a program needn't handle non-finite values.
Results may differ from a plain program's by a relative error of at most 0.0071.
Values may be sent and summed in bfloat16 or wider, within the bound.
A program may use at most 64 MiB of HBM per device.

v0:
```python
import math
import jax
import jax.numpy as jnp
from jax import lax
from jax.sharding import PartitionSpec as P

INV_ROOT_TWO = 0.7071067811865476
INV_ROOT_TAU = 0.3989422804014327


def from_behind(block, axis, distance):
    devices = range(lax.axis_size(axis))
    route = [(i - distance, i) for i in devices if i - distance in devices]
    return lax.ppermute(block, axis, route)


def gelu_value(pre_act):
    return 0.5 * pre_act * (1.0 + jax.scipy.special.erf(pre_act * INV_ROOT_TWO))


def gelu_slope(pre_act):
    return (
        0.5 * (1.0 + jax.scipy.special.erf(pre_act * INV_ROOT_TWO))
        + pre_act * jnp.exp(-0.5 * pre_act * pre_act) * INV_ROOT_TAU
    )


def spatial_pad(field_in):
    pad_spec = [(0, 0)] * (field_in.ndim - 3) + [(1, 1), (1, 1), (0, 0)]
    return jnp.pad(field_in, pad_spec)


def spatial(field_in, kernel):
    height, width = (field_in.shape[-3], field_in.shape[-2])
    padded = spatial_pad(field_in)
    summed = jnp.zeros_like(field_in)
    for row_off in range(3):
        for col_off in range(3):
            summed = (
                summed
                + kernel[3 * row_off + col_off]
                * padded[..., row_off : row_off + height, col_off : col_off + width, :]
            )
    return summed


def spatial_back(grad_in, kernel):
    height, width = (grad_in.shape[-3], grad_in.shape[-2])
    padded = spatial_pad(grad_in)
    summed = jnp.zeros_like(grad_in)
    for row_off in range(3):
        for col_off in range(3):
            summed = (
                summed
                + kernel[3 * row_off + col_off]
                * padded[
                    ..., 2 - row_off : 2 - row_off + height, 2 - col_off : 2 - col_off + width, :
                ]
            )
    return summed


def spatial_kernel_grad(field_in, grad_in):
    height, width = (field_in.shape[-3], field_in.shape[-2])
    padded = spatial_pad(field_in)
    axes_all = tuple(range(field_in.ndim - 1))
    parts = []
    for row_off in range(3):
        for col_off in range(3):
            parts.append(
                jnp.sum(
                    padded[..., row_off : row_off + height, col_off : col_off + width, :] * grad_in,
                    axis=axes_all,
                )
            )
    return jnp.stack(parts)


def front_pad(field_in, tap_count):
    pad_spec = [(0, 0)] * (field_in.ndim - 4) + [(tap_count - 1, 0), (0, 0), (0, 0), (0, 0)]
    return jnp.pad(field_in, pad_spec)


def temporal(field_in, kernel):
    tap_count = kernel.shape[0]
    frames = field_in.shape[-4]
    padded = front_pad(field_in, tap_count)
    summed = jnp.zeros_like(field_in)
    for delay in range(tap_count):
        first = tap_count - 1 - delay
        summed = summed + kernel[delay] * padded[..., first : first + frames, :, :, :]
    return summed


def temporal_back(grad_in, kernel):
    tap_count = kernel.shape[0]
    frames = grad_in.shape[-4]
    pad_spec = [(0, 0)] * (grad_in.ndim - 4) + [(0, tap_count - 1), (0, 0), (0, 0), (0, 0)]
    padded = jnp.pad(grad_in, pad_spec)
    summed = jnp.zeros_like(grad_in)
    for delay in range(tap_count):
        summed = summed + kernel[delay] * padded[..., delay : delay + frames, :, :, :]
    return summed


def temporal_kernel_grad(field_in, grad_in, tap_count):
    frames = field_in.shape[-4]
    padded = front_pad(field_in, tap_count)
    axes_all = tuple(range(field_in.ndim - 1))
    parts = []
    for delay in range(tap_count):
        first = tap_count - 1 - delay
        parts.append(jnp.sum(padded[..., first : first + frames, :, :, :] * grad_in, axis=axes_all))
    return jnp.stack(parts)


def section_back(inputs, grad_out, s_kernel, t_kernel, hidden_of):
    field_in = inputs.astype(jnp.float32)
    spread = spatial(field_in, s_kernel)
    pre_act = temporal(spread, t_kernel)
    hidden = gelu_value(pre_act).astype(jnp.bfloat16)
    channels = inputs.shape[-1]
    flat_grad = grad_out.reshape(-1, channels)
    flat_hidden = hidden.reshape(-1, channels)
    hidden_grad = hidden_of(flat_grad).reshape(pre_act.shape)
    pre_grad = hidden_grad * gelu_slope(pre_act)
    spread_grad = temporal_back(pre_grad, t_kernel)
    in_grad = (grad_out.astype(jnp.float32) + spatial_back(spread_grad, s_kernel)).astype(
        jnp.bfloat16
    )
    weight_grad = jnp.dot(flat_hidden.T, flat_grad, preferred_element_type=jnp.float32)
    s_part = spatial_kernel_grad(field_in, spread_grad)
    t_part = temporal_kernel_grad(spread, pre_grad, t_kernel.shape[0])
    return (in_grad, weight_grad, s_part, t_part)


def local(
    section_inputs, cotangent, sessions, point_weight, spatial_kernel, temporal_kernel, readout
):
    section_count = lax.axis_size("section")
    my_section = lax.axis_index("section")
    inputs = section_inputs[0]
    s_kernel = spatial_kernel[0]
    t_kernel = temporal_kernel[0]
    weight_shard = point_weight[0]
    clip_count = inputs.shape[0]
    channels = inputs.shape[-1]
    chosen = jnp.take(readout, sessions, axis=0)
    top_grads = jnp.einsum(
        "cfhwr,crk->cfhwk", cotangent, chosen, preferred_element_type=jnp.float32
    ).astype(jnp.bfloat16)
    block_size = 2
    step_count = clip_count // block_size
    tick_count = step_count + section_count - 1
    full_weight = lax.all_gather(weight_shard, "dp", axis=0, tiled=True)

    def hidden_of(flat_grad):
        return jnp.dot(flat_grad, full_weight.T, preferred_element_type=jnp.float32)

    block_shape = (block_size,) + inputs.shape[1:]

    def tick(tick_index, state_now):
        incoming, w_sum, s_sum, t_sum = state_now
        clip_step = tick_index - (section_count - 1 - my_section)
        is_live = (clip_step >= 0) & (clip_step < step_count)
        first_clip = jnp.clip(clip_step, 0, step_count - 1) * block_size
        inputs_block = lax.dynamic_slice_in_dim(inputs, first_clip, block_size, 0)
        top_block = lax.dynamic_slice_in_dim(top_grads, first_clip, block_size, 0)
        grad_out = jnp.where(my_section == section_count - 1, top_block, incoming)

        def live_work(sums):
            in_grad, w_part, s_part, t_part = section_back(
                inputs_block, grad_out, s_kernel, t_kernel, hidden_of
            )
            return (in_grad, sums[0] + w_part, sums[1] + s_part, sums[2] + t_part)

        def dead_work(sums):
            return (jnp.zeros(block_shape, jnp.bfloat16), sums[0], sums[1], sums[2])

        in_grad, w_new, s_new, t_new = lax.cond(
            is_live, live_work, dead_work, (w_sum, s_sum, t_sum)
        )
        passed = from_behind(in_grad, "section", -1)
        return (passed, w_new, s_new, t_new)

    start_state = (
        jnp.zeros(block_shape, jnp.bfloat16),
        jnp.zeros((channels, channels), jnp.float32),
        jnp.zeros((9, channels), jnp.float32),
        jnp.zeros(t_kernel.shape, jnp.float32),
    )
    finals = lax.fori_loop(0, tick_count, tick, start_state)
    weight_grads = lax.psum_scatter(finals[1], "dp", scatter_dimension=0, tiled=True)
    s_total, t_total = lax.psum((finals[2], finals[3]), "dp")
    rows_all = (
        clip_count * lax.axis_size("dp") * inputs.shape[1] * inputs.shape[2] * inputs.shape[3]
    )
    factor = 1.0 / math.sqrt(rows_all)
    return ((weight_grads * factor)[None], (s_total * factor)[None], (t_total * factor)[None])


def solution(mesh):
    return jax.shard_map(
        local,
        mesh=mesh,
        in_specs=(
            P("section", "dp", None, None, None, None),
            P("dp", None, None, None, None),
            P("dp"),
            P("section", "dp", None),
            P("section", None, None),
            P("section", None, None),
            P(),
        ),
        out_specs=(P("section", "dp", None), P("section", None, None), P("section", None, None)),
        check_vma=False,
    )
```

profile of v0, /device:TPU:0, one launch (start us, length us, event | category | flops | bytes accessed | tf_op | source)
XLA Modules:
  0.0 254.5 jit_solution(1457571173146096510)
XLA Ops:
  10.7 3.1 %copy.22 = bf16[1,8,8,4,4,768]{5,2,4,3,1,0:T(8,128)(2,1)} copy(bf16[1,8,8,4,4,768]{5,4,3,2,1,0:T(4,128)(2,1)} %param.11) | data formatting | bytes 3145728 | tf_op args[0]
  16.5 34.8 %all-gather.3.cloned.1.call-done = bf16[1,768,768]{2,1,0:T(8,128)(2,1)} async-done(((bf16[1,48,768]{2,1,0:T(8,128)(2,1)}), bf16[1,768,768]{2,1,0:T(8,128)(2,1)}) %all-gather.3.cloned.1.call-update) | async-done | bytes 1179664 | tf_op jit(solution)/shard_map/all_gather | solution.py:155
  54.2 130.3 %while.21 = (s32[]{:T(128)}, bf16[2,8,4,4,768]{4,1,3,2,0:T(8,128)(2,1)S(1)}, f32[768,768]{1,0:T(8,128)}, f32[9,768]{1,0:T(8,128)}, f32[5,768]{1,0:T(8,128)}, /*i...) while((s32[]{:T(128)}, ...), condition=%wide.region_17.18_spmd, body=%wide.region_0.17_spmd.sunk | while | flops 625999872 | bytes 24124888 | solution.py:192
  55.5 25.5 %collective-permute-done = bf16[2,8,4,4,768]{4,1,3,2,0:T(8,128)(2,1)S(1)} collective-permute-done((bf16[2,8,4,4,768]{4,1,3,2,0:T(8,128)(2,1)S(1)}, bf16[2,8,4,4,768]{4,1,3,2,0:T(8,128)(2,1)S(1)}, u32[]{:S(2)}, u32[]{:S(2)}) %collective-permute-start) | collective-permute-done | bytes 393248 | tf_op jit(solution)/shard_map/while/body/eval_jaxpr/ppermute | solution.py:14
  81.0 14.6 %conditional.2 = (bf16[2,8,4,4,768]{4,1,3,2,0:T(8,128)(2,1)S(1)}, f32[768,768]{1,0:T(8,128)}, f32[9,768]{1,0:T(8,128)}, f32[5,768]{1,0:T(8,128)}) conditional(s32[]{:T(128)} %convert_element_type.67, (f32[768,768]{1,0:T(8,128)}, f32[9,768]{1,0:T(8,128)}, f32[5,768]{1,0:T(8,128)}) %tuple.101, (pred[]{:T(512)}, s32[]{:T(128)}, ...), branch_computations={%region_1.1_spmd, %region_2.16_spmd} | conditional | flops 625999872 | bytes 22551692 | solution.py:180
  83.9 2.1 multiply_reduce_fusion
  86.0 1.9 multiply_reduce_fusion.5
  91.5 4.1 %bitcast_add_fusion = f32[768,768]{1,0:T(8,128)} fusion(f32[768,768]{1,0:T(8,128)} %get-tuple-element.418, bf16[2,8,4,4,768]{4,1,3,2,0:T(8,128)(2,1)S(1)} %get-tuple-element.504, f32[2,8,4,4,768]{4,1,3,2,0:T(8,128)S(1)} %multiply_add_fusion.1, f32[768]{0:T(1024)S(1)} %get-tuple-element.471, f32[768]{0:T(1024)S(1)} %get-tuple-element.472, ...), kind=kOutput, calls=%fused_computation.25 | convolution fusion | flops 305332224 | bytes 5913600 | tf_op jit(solution)/shard_map/while/body/eval_jaxpr/cond/branch_1_fun/dot_general | solution.py:131
  96.9 11.4 %collective-permute-done = bf16[2,8,4,4,768]{4,1,3,2,0:T(8,128)(2,1)S(1)} collective-permute-done((bf16[2,8,4,4,768]{4,1,3,2,0:T(8,128)(2,1)S(1)}, bf16[2,8,4,4,768]{4,1,3,2,0:T(8,128)(2,1)S(1)}, u32[]{:S(2)}, u32[]{:S(2)}) %collective-permute-start) | collective-permute-done | bytes 393248 | tf_op jit(solution)/shard_map/while/body/eval_jaxpr/ppermute | solution.py:14
  108.2 14.6 %conditional.2 = (bf16[2,8,4,4,768]{4,1,3,2,0:T(8,128)(2,1)S(1)}, f32[768,768]{1,0:T(8,128)}, f32[9,768]{1,0:T(8,128)}, f32[5,768]{1,0:T(8,128)}) conditional(s32[]{:T(128)} %convert_element_type.67, (f32[768,768]{1,0:T(8,128)}, f32[9,768]{1,0:T(8,128)}, f32[5,768]{1,0:T(8,128)}) %tuple.101, (pred[]{:T(512)}, s32[]{:T(128)}, ...), branch_computations={%region_1.1_spmd, %region_2.16_spmd} | conditional | flops 625999872 | bytes 22551692 | solution.py:180
  111.2 2.1 multiply_reduce_fusion
  113.2 1.9 multiply_reduce_fusion.5
  118.7 4.1 %bitcast_add_fusion = f32[768,768]{1,0:T(8,128)} fusion(f32[768,768]{1,0:T(8,128)} %get-tuple-element.418, bf16[2,8,4,4,768]{4,1,3,2,0:T(8,128)(2,1)S(1)} %get-tuple-element.504, f32[2,8,4,4,768]{4,1,3,2,0:T(8,128)S(1)} %multiply_add_fusion.1, f32[768]{0:T(1024)S(1)} %get-tuple-element.471, f32[768]{0:T(1024)S(1)} %get-tuple-element.472, ...), kind=kOutput, calls=%fused_computation.25 | convolution fusion | flops 305332224 | bytes 5913600 | tf_op jit(solution)/shard_map/while/body/eval_jaxpr/cond/branch_1_fun/dot_general | solution.py:131
  124.1 10.5 %collective-permute-done = bf16[2,8,4,4,768]{4,1,3,2,0:T(8,128)(2,1)S(1)} collective-permute-done((bf16[2,8,4,4,768]{4,1,3,2,0:T(8,128)(2,1)S(1)}, bf16[2,8,4,4,768]{4,1,3,2,0:T(8,128)(2,1)S(1)}, u32[]{:S(2)}, u32[]{:S(2)}) %collective-permute-start) | collective-permute-done | bytes 393248 | tf_op jit(solution)/shard_map/while/body/eval_jaxpr/ppermute | solution.py:14
  134.6 14.6 %conditional.2 = (bf16[2,8,4,4,768]{4,1,3,2,0:T(8,128)(2,1)S(1)}, f32[768,768]{1,0:T(8,128)}, f32[9,768]{1,0:T(8,128)}, f32[5,768]{1,0:T(8,128)}) conditional(s32[]{:T(128)} %convert_element_type.67, (f32[768,768]{1,0:T(8,128)}, f32[9,768]{1,0:T(8,128)}, f32[5,768]{1,0:T(8,128)}) %tuple.101, (pred[]{:T(512)}, s32[]{:T(128)}, ...), branch_computations={%region_1.1_spmd, %region_2.16_spmd} | conditional | flops 625999872 | bytes 22551692 | solution.py:180
  137.5 2.1 multiply_reduce_fusion
  145.0 4.1 %bitcast_add_fusion = f32[768,768]{1,0:T(8,128)} fusion(f32[768,768]{1,0:T(8,128)} %get-tuple-element.418, bf16[2,8,4,4,768]{4,1,3,2,0:T(8,128)(2,1)S(1)} %get-tuple-element.504, f32[2,8,4,4,768]{4,1,3,2,0:T(8,128)S(1)} %multiply_add_fusion.1, f32[768]{0:T(1024)S(1)} %get-tuple-element.471, f32[768]{0:T(1024)S(1)} %get-tuple-element.472, ...), kind=kOutput, calls=%fused_computation.25 | convolution fusion | flops 305332224 | bytes 5913600 | tf_op jit(solution)/shard_map/while/body/eval_jaxpr/cond/branch_1_fun/dot_general | solution.py:131
  150.4 9.6 %collective-permute-done = bf16[2,8,4,4,768]{4,1,3,2,0:T(8,128)(2,1)S(1)} collective-permute-done((bf16[2,8,4,4,768]{4,1,3,2,0:T(8,128)(2,1)S(1)}, bf16[2,8,4,4,768]{4,1,3,2,0:T(8,128)(2,1)S(1)}, u32[]{:S(2)}, u32[]{:S(2)}) %collective-permute-start) | collective-permute-done | bytes 393248 | tf_op jit(solution)/shard_map/while/body/eval_jaxpr/ppermute | solution.py:14
  160.0 14.6 %conditional.2 = (bf16[2,8,4,4,768]{4,1,3,2,0:T(8,128)(2,1)S(1)}, f32[768,768]{1,0:T(8,128)}, f32[9,768]{1,0:T(8,128)}, f32[5,768]{1,0:T(8,128)}) conditional(s32[]{:T(128)} %convert_element_type.67, (f32[768,768]{1,0:T(8,128)}, f32[9,768]{1,0:T(8,128)}, f32[5,768]{1,0:T(8,128)}) %tuple.101, (pred[]{:T(512)}, s32[]{:T(128)}, ...), branch_computations={%region_1.1_spmd, %region_2.16_spmd} | conditional | flops 625999872 | bytes 22551692 | solution.py:180
  162.9 2.1 multiply_reduce_fusion
  165.0 1.9 multiply_reduce_fusion.5
  170.4 4.1 %bitcast_add_fusion = f32[768,768]{1,0:T(8,128)} fusion(f32[768,768]{1,0:T(8,128)} %get-tuple-element.418, bf16[2,8,4,4,768]{4,1,3,2,0:T(8,128)(2,1)S(1)} %get-tuple-element.504, f32[2,8,4,4,768]{4,1,3,2,0:T(8,128)S(1)} %multiply_add_fusion.1, f32[768]{0:T(1024)S(1)} %get-tuple-element.471, f32[768]{0:T(1024)S(1)} %get-tuple-element.472, ...), kind=kOutput, calls=%fused_computation.25 | convolution fusion | flops 305332224 | bytes 5913600 | tf_op jit(solution)/shard_map/while/body/eval_jaxpr/cond/branch_1_fun/dot_general | solution.py:131
  175.8 8.6 %collective-permute-done = bf16[2,8,4,4,768]{4,1,3,2,0:T(8,128)(2,1)S(1)} collective-permute-done((bf16[2,8,4,4,768]{4,1,3,2,0:T(8,128)(2,1)S(1)}, bf16[2,8,4,4,768]{4,1,3,2,0:T(8,128)(2,1)S(1)}, u32[]{:S(2)}, u32[]{:S(2)}) %collective-permute-start) | collective-permute-done | bytes 393248 | tf_op jit(solution)/shard_map/while/body/eval_jaxpr/ppermute | solution.py:14
  184.5 59.6 %all-reduce.4 = (f32[9,768]{1,0:T(8,128)S(1)}, f32[5,768]{1,0:T(8,128)S(1)}) all-reduce(f32[9,768]{1,0:T(8,128)} %get-tuple-element.445, f32[5,768]{1,0:T(8,128)} %get-tuple-element.446), channel_id=1, replica_groups=mesh['dp'=16,'section'=2] {'dp'}, use_global_device_ids=true, to_apply=%region_19.20 | all-reduce | flops 10752 | bytes 86016 | tf_op jit(solution)/shard_map/psum | solution.py:194
  (131 shorter events, 46.3 us)
Async XLA Ops:
  7.2 6.6 %copy-start = (bf16[4,128,768]{2,1,0:T(8,128)(2,1)S(1)}, bf16[4,128,768]{2,1,0:T(8,128)(2,1)}, u32[]{:S(2)}) copy-start(bf16[4,128,768]{2,1,0:T(8,128)(2,1)} %param.17) | copy-start | bytes 2359300
  7.2 44.2 %all-gather.3.cloned.1.call-start = ((), (), s32[]{:S(2)}) async-start(), calls=%async_computation.2 | async-start | bytes 1253376 | tf_op jit(solution)/shard_map/all_gather | solution.py:155
  7.9 238.1 %reduce-scatter.2.cloned.1.call-start = ((), (), s32[]{:S(2)}) async-start(), calls=%async_computation.1 | async-start | bytes 2506752 | tf_op jit(solution)/shard_map/reduce_scatter | solution.py:193
  10.7 3.1 %copy-start.3 = (s32[8]{0:T(128)S(1)}, s32[8]{0:T(128)}, u32[]{:S(2)}) copy-start(s32[8]{0:T(128)} %param.13) | copy-start | bytes 100
  13.8 1.0 copy-start.2
  54.2 26.8 %collective-permute-start = (bf16[2,8,4,4,768]{4,1,3,2,0:T(8,128)(2,1)S(1)}, bf16[2,8,4,4,768]{4,1,3,2,0:T(8,128)(2,1)S(1)}, u32[]{:S(2)}, u32[]{:S(2)}) collective-permute-start(bf16[2,8,4,4,768]{4,1,3,2,0:T(8,128)(2,1)S(1)} %get-tuple-element.591), channel_id=1, source_target_pairs={{1,0},{3,2},{5,4},{7,6},{9,8},{11,10},{13,12},{15,14},{17,16},{19,... | collective-permute-start | bytes 1179656 | tf_op jit(solution)/shard_map/while/body/eval_jaxpr/ppermute | solution.py:14
  81.0 2.9 %copy-start.1 = (bf16[768,768]{1,0:T(8,128)(2,1)S(1)}, bf16[768,768]{1,0:T(8,128)(2,1)}, u32[]{:S(2)}) copy-start(bf16[768,768]{1,0:T(8,128)(2,1)} %get-tuple-element.416) | copy-start | bytes 3538948 | tf_op jit(solution)/shard_map/while/body/eval_jaxpr/cond
  95.6 12.7 %collective-permute-start = (bf16[2,8,4,4,768]{4,1,3,2,0:T(8,128)(2,1)S(1)}, bf16[2,8,4,4,768]{4,1,3,2,0:T(8,128)(2,1)S(1)}, u32[]{:S(2)}, u32[]{:S(2)}) collective-permute-start(bf16[2,8,4,4,768]{4,1,3,2,0:T(8,128)(2,1)S(1)} %get-tuple-element.591), channel_id=1, source_target_pairs={{1,0},{3,2},{5,4},{7,6},{9,8},{11,10},{13,12},{15,14},{17,16},{19,... | collective-permute-start | bytes 1179656 | tf_op jit(solution)/shard_map/while/body/eval_jaxpr/ppermute | solution.py:14
  108.2 2.9 %copy-start.1 = (bf16[768,768]{1,0:T(8,128)(2,1)S(1)}, bf16[768,768]{1,0:T(8,128)(2,1)}, u32[]{:S(2)}) copy-start(bf16[768,768]{1,0:T(8,128)(2,1)} %get-tuple-element.416) | copy-start | bytes 3538948 | tf_op jit(solution)/shard_map/while/body/eval_jaxpr/cond
  122.8 11.8 %collective-permute-start = (bf16[2,8,4,4,768]{4,1,3,2,0:T(8,128)(2,1)S(1)}, bf16[2,8,4,4,768]{4,1,3,2,0:T(8,128)(2,1)S(1)}, u32[]{:S(2)}, u32[]{:S(2)}) collective-permute-start(bf16[2,8,4,4,768]{4,1,3,2,0:T(8,128)(2,1)S(1)} %get-tuple-element.591), channel_id=1, source_target_pairs={{1,0},{3,2},{5,4},{7,6},{9,8},{11,10},{13,12},{15,14},{17,16},{19,... | collective-permute-start | bytes 1179656 | tf_op jit(solution)/shard_map/while/body/eval_jaxpr/ppermute | solution.py:14
  134.6 2.9 %copy-start.1 = (bf16[768,768]{1,0:T(8,128)(2,1)S(1)}, bf16[768,768]{1,0:T(8,128)(2,1)}, u32[]{:S(2)}) copy-start(bf16[768,768]{1,0:T(8,128)(2,1)} %get-tuple-element.416) | copy-start | bytes 3538948 | tf_op jit(solution)/shard_map/while/body/eval_jaxpr/cond
  149.1 10.9 %collective-permute-start = (bf16[2,8,4,4,768]{4,1,3,2,0:T(8,128)(2,1)S(1)}, bf16[2,8,4,4,768]{4,1,3,2,0:T(8,128)(2,1)S(1)}, u32[]{:S(2)}, u32[]{:S(2)}) collective-permute-start(bf16[2,8,4,4,768]{4,1,3,2,0:T(8,128)(2,1)S(1)} %get-tuple-element.591), channel_id=1, source_target_pairs={{1,0},{3,2},{5,4},{7,6},{9,8},{11,10},{13,12},{15,14},{17,16},{19,... | collective-permute-start | bytes 1179656 | tf_op jit(solution)/shard_map/while/body/eval_jaxpr/ppermute | solution.py:14
  160.0 2.9 %copy-start.1 = (bf16[768,768]{1,0:T(8,128)(2,1)S(1)}, bf16[768,768]{1,0:T(8,128)(2,1)}, u32[]{:S(2)}) copy-start(bf16[768,768]{1,0:T(8,128)(2,1)} %get-tuple-element.416) | copy-start | bytes 3538948 | tf_op jit(solution)/shard_map/while/body/eval_jaxpr/cond
  174.5 9.9 %collective-permute-start = (bf16[2,8,4,4,768]{4,1,3,2,0:T(8,128)(2,1)S(1)}, bf16[2,8,4,4,768]{4,1,3,2,0:T(8,128)(2,1)S(1)}, u32[]{:S(2)}, u32[]{:S(2)}) collective-permute-start(bf16[2,8,4,4,768]{4,1,3,2,0:T(8,128)(2,1)S(1)} %get-tuple-element.591), channel_id=1, source_target_pairs={{1,0},{3,2},{5,4},{7,6},{9,8},{11,10},{13,12},{15,14},{17,16},{19,... | collective-permute-start | bytes 1179656 | tf_op jit(solution)/shard_map/while/body/eval_jaxpr/ppermute | solution.py:14
Sparse Core Ops, SparseCore 0:
  10.3 41.0 all-gather.2
  184.6 61.4 reduce-scatter.1
where the time goes:
time: 256 us; the launch traced here: 254 us
  waiting for transfers between devices  102 us (40%)
  blocking collectives  59.6 us (23%)
  other arithmetic  28.9 us (11%)
  matrix products  26.5 us (10%)
  local copies, waits for them, and re-layouts  16.4 us (6%)
  between operations  14.1 us (6%)
  starting transfers between devices  6.49 us (3%)
    ppermute x5, waiting for transfers between devices, from_behind(): return lax.ppermute(block, axis, route)  65.5 us
    psum x1, blocking collectives, local(): s_total, t_total = lax.psum((finals[2], finals[3]), 'dp')  59.6 us
    all_gather x1, waiting for transfers between devices, local(): full_weight = lax.all_gather(weight_shard, 'dp', axis=0, tiled=True)  34.8 us
    dot_general x4, matrix products, section_back(): jnp.dot(flat_hidden.T, flat_grad, preferred_element_type=jnp.float32)  16.4 us
    add x8, other arithmetic, live_work(): return (in_grad, sums[0] + w_part, sums[1] + s_part, sums[2] + t_part)  11.1 us
    dot_general x4, matrix products, hidden_of(): return jnp.dot(flat_grad, full_weight.T, preferred_element_type=jnp.float32)  8.29 us
    reduce_sum x4, other arithmetic, spatial_kernel_grad(): jnp.sum(padded[..., row_off:row_off + height, col_off:col_off + width, :]...  7.66 us
    ppermute x5, starting transfers between devices, from_behind(): return lax.ppermute(block, axis, route)  6.41 us
  transfers between devices with their start and end apart: 7, of which 7 were waited for; matrix products, arithmetic and copies ran while one was open for 4% of the time, Pallas kernels for 0%

commit v1 on v0

--- a/solution.py
+++ b/solution.py
@@ -152,7 +152,15 @@
     block_size = 2
     step_count = clip_count // block_size
     tick_count = step_count + section_count - 1
-    full_weight = lax.all_gather(weight_shard, "dp", axis=0, tiled=True)
+    ways, here = (lax.axis_size("dp"), lax.axis_index("dp"))
+    grown, reach = (weight_shard, 1)
+    while reach < ways:
+        theirs = lax.ppermute(grown, "dp", [(d, d ^ reach) for d in range(ways)])
+        mine_first = jnp.concatenate([grown, theirs], axis=0)
+        theirs_first = jnp.concatenate([theirs, grown], axis=0)
+        grown = jnp.where(here & reach == 0, mine_first, theirs_first)
+        reach = 2 * reach
+    full_weight = grown
 
     def hidden_of(flat_grad):
         return jnp.dot(flat_grad, full_weight.T, preferred_element_type=jnp.float32)

time: 256 us -> 261 us (1.020)
  waiting for transfers between devices: 102 us -> 93.5 us
  starting transfers between devices: 6.49 us -> 14.2 us
  blocking collectives: 59.6 us -> 63 us
  other arithmetic: 28.9 us -> 31.7 us
    all_gather x1 -> x0, waiting for transfers between devices: 34.8 us -> none  [local(): full_weight = lax.all_gather(weight_shard, 'dp', axis=0, tiled=True)]
    ppermute x0 -> x4, waiting for transfers between devices: none -> 31 us  [local(): theirs = lax.ppermute(grown, 'dp', [(d, d ^ reach) for d in range(ways)])]
    ppermute x0 -> x4, starting transfers between devices: none -> 7.72 us  [local(): theirs = lax.ppermute(grown, 'dp', [(d, d ^ reach) for d in range(ways)])]
    ppermute x5, waiting for transfers between devices: 65.5 us -> 59.8 us  [from_behind(): return lax.ppermute(block, axis, route)]
    psum x1, blocking collectives: 59.6 us -> 63 us  [local(): s_total, t_total = lax.psum((finals[2], finals[3]), 'dp')]
    select_n x0 -> x4, other arithmetic: none -> 2.72 us  [local(): grown = jnp.where(here & reach == 0, mine_first, theirs_first)]
  transfers between devices with their start and end apart: 7 -> 10, of which waited for: 7 -> 9; matrix products, arithmetic and copies ran while one was open for 4% -> 4% of each run, Pallas kernels for 0% -> 0%
where the time goes in v1:
time: 261 us; the launch traced here: 260 us
  waiting for transfers between devices  93.5 us (36%)
  blocking collectives  63 us (24%)
  other arithmetic  31.7 us (12%)
  matrix products  26.5 us (10%)
  local copies, waits for them, and re-layouts  16.2 us (6%)
  starting transfers between devices  14.2 us (5%)
  between operations  14.1 us (5%)
    psum x1, blocking collectives, local(): s_total, t_total = lax.psum((finals[2], finals[3]), 'dp')  63 us
    ppermute x5, waiting for transfers between devices, from_behind(): return lax.ppermute(block, axis, route)  59.8 us
    ppermute x4, waiting for transfers between devices, local(): theirs = lax.ppermute(grown, 'dp', [(d, d ^ reach) for d in range(ways)])  31 us
    dot_general x4, matrix products, section_back(): jnp.dot(flat_hidden.T, flat_grad, preferred_element_type=jnp.float32)  16.4 us
    add x8, other arithmetic, live_work(): return (in_grad, sums[0] + w_part, sums[1] + s_part, sums[2] + t_part)  11.1 us
    dot_general x4, matrix products, hidden_of(): return jnp.dot(flat_grad, full_weight.T, preferred_element_type=jnp.float32)  8.3 us
    ppermute x4, starting transfers between devices, local(): theirs = lax.ppermute(grown, 'dp', [(d, d ^ reach) for d in range(ways)])  7.72 us
    reduce_sum x4, other arithmetic, spatial_kernel_grad(): jnp.sum(padded[..., row_off:row_off + height, col_off:col_off + width, :]...  7.66 us
  transfers between devices with their start and end apart: 10, of which 9 were waited for; matrix products, arithmetic and copies ran while one was open for 4% of the time, Pallas kernels for 0%

profile of v1, /device:TPU:0, one launch (start us, length us, event | category | flops | bytes accessed | tf_op | source)
XLA Modules:
  0.0 259.8 jit_solution(4412056679863201709)
XLA Ops:
  9.9 2.9 %collective-permute-start.2 = (bf16[96,768]{1,0:T(8,128)(2,1)S(1)}, bf16[96,768]{1,0:T(8,128)(2,1)S(1)}, u32[]{:S(2)}, u32[]{:S(2)}) collective-permute-start(bf16[96,768]{1,0:T(8,128)(2,1)S(1)} %maximum_select_fusion.3), channel_id=1, source_target_pairs={{0,4},{2,6},{4,0},{6,2},{8,12},{10,14},{12,8},{14,10},{16,20},{18,... | collective-permute-start | bytes 442376 | tf_op jit(solution)/shard_map/ppermute | solution.py:158
  15.5 3.1 %copy.22 = bf16[1,8,8,4,4,768]{5,2,4,3,1,0:T(8,128)(2,1)} copy(bf16[1,8,8,4,4,768]{5,4,3,2,1,0:T(4,128)(2,1)} %param.11) | data formatting | bytes 3145728 | tf_op args[0]
  20.9 6.5 %collective-permute-done.3 = bf16[192,768]{1,0:T(8,128)(2,1)S(1)} collective-permute-done((bf16[192,768]{1,0:T(8,128)(2,1)S(1)}, bf16[192,768]{1,0:T(8,128)(2,1)S(1)}, u32[]{:S(2)}, u32[]{:S(2)}) %collective-permute-start.3) | collective-permute-done | bytes 294944 | tf_op jit(solution)/shard_map/ppermute | solution.py:158
  27.7 2.7 %collective-permute-start.4 = (bf16[384,768]{1,0:T(8,128)(2,1)S(1)}, bf16[384,768]{1,0:T(8,128)(2,1)S(1)}, u32[]{:S(2)}, u32[]{:S(2)}) collective-permute-start(bf16[384,768]{1,0:T(8,128)(2,1)S(1)} %maximum_select_fusion.1), channel_id=1, source_target_pairs={{0,16},{2,18},{4,20},{6,22},{8,24},{10,26},{12,28},{14,30},{16,0},... | collective-permute-start | bytes 1769480 | tf_op jit(solution)/shard_map/ppermute | solution.py:158
  32.1 23.4 %collective-permute-done.4 = bf16[384,768]{1,0:T(8,128)(2,1)S(1)} collective-permute-done((bf16[384,768]{1,0:T(8,128)(2,1)S(1)}, bf16[384,768]{1,0:T(8,128)(2,1)S(1)}, u32[]{:S(2)}, u32[]{:S(2)}) %collective-permute-start.4) | collective-permute-done | bytes 589856 | tf_op jit(solution)/shard_map/ppermute | solution.py:158
  59.8 124.6 %while.21 = (s32[]{:T(128)}, bf16[2,8,4,4,768]{4,1,3,2,0:T(8,128)(2,1)S(1)}, f32[768,768]{1,0:T(8,128)}, f32[9,768]{1,0:T(8,128)}, f32[5,768]{1,0:T(8,128)}, /*i...) while((s32[]{:T(128)}, ...), condition=%wide.region_17.18_spmd, body=%wide.region_0.17_spmd.sunk | while | flops 625999872 | bytes 24124888 | solution.py:200
  61.2 24.2 %collective-permute-done = bf16[2,8,4,4,768]{4,1,3,2,0:T(8,128)(2,1)S(1)} collective-permute-done((bf16[2,8,4,4,768]{4,1,3,2,0:T(8,128)(2,1)S(1)}, bf16[2,8,4,4,768]{4,1,3,2,0:T(8,128)(2,1)S(1)}, u32[]{:S(2)}, u32[]{:S(2)}) %collective-permute-start) | collective-permute-done | bytes 393248 | tf_op jit(solution)/shard_map/while/body/eval_jaxpr/ppermute | solution.py:14
  85.4 14.6 %conditional.2 = (bf16[2,8,4,4,768]{4,1,3,2,0:T(8,128)(2,1)S(1)}, f32[768,768]{1,0:T(8,128)}, f32[9,768]{1,0:T(8,128)}, f32[5,768]{1,0:T(8,128)}) conditional(s32[]{:T(128)} %convert_element_type.67, (f32[768,768]{1,0:T(8,128)}, f32[9,768]{1,0:T(8,128)}, f32[5,768]{1,0:T(8,128)}) %tuple.101, (pred[]{:T(512)}, s32[]{:T(128)}, ...), branch_computations={%region_1.1_spmd, %region_2.16_spmd} | conditional | flops 625999872 | bytes 22551692 | solution.py:188
  95.8 4.1 %bitcast_add_fusion = f32[768,768]{1,0:T(8,128)} fusion(f32[768,768]{1,0:T(8,128)} %get-tuple-element.418, bf16[2,8,4,4,768]{4,1,3,2,0:T(8,128)(2,1)S(1)} %get-tuple-element.504, f32[2,8,4,4,768]{4,1,3,2,0:T(8,128)S(1)} %multiply_add_fusion.1, f32[768]{0:T(1024)S(1)} %get-tuple-element.471, f32[768]{0:T(1024)S(1)} %get-tuple-element.472, ...), kind=kOutput, calls=%fused_computation.25 | convolution fusion | flops 305332224 | bytes 5913600 | tf_op jit(solution)/shard_map/while/body/eval_jaxpr/cond/branch_1_fun/dot_general | solution.py:131
  101.2 9.9 %collective-permute-done = bf16[2,8,4,4,768]{4,1,3,2,0:T(8,128)(2,1)S(1)} collective-permute-done((bf16[2,8,4,4,768]{4,1,3,2,0:T(8,128)(2,1)S(1)}, bf16[2,8,4,4,768]{4,1,3,2,0:T(8,128)(2,1)S(1)}, u32[]{:S(2)}, u32[]{:S(2)}) %collective-permute-start) | collective-permute-done | bytes 393248 | tf_op jit(solution)/shard_map/while/body/eval_jaxpr/ppermute | solution.py:14
  111.1 14.6 %conditional.2 = (bf16[2,8,4,4,768]{4,1,3,2,0:T(8,128)(2,1)S(1)}, f32[768,768]{1,0:T(8,128)}, f32[9,768]{1,0:T(8,128)}, f32[5,768]{1,0:T(8,128)}) conditional(s32[]{:T(128)} %convert_element_type.67, (f32[768,768]{1,0:T(8,128)}, f32[9,768]{1,0:T(8,128)}, f32[5,768]{1,0:T(8,128)}) %tuple.101, (pred[]{:T(512)}, s32[]{:T(128)}, ...), branch_computations={%region_1.1_spmd, %region_2.16_spmd} | conditional | flops 625999872 | bytes 22551692 | solution.py:188
  114.1 2.1 multiply_reduce_fusion
  121.6 4.1 %bitcast_add_fusion = f32[768,768]{1,0:T(8,128)} fusion(f32[768,768]{1,0:T(8,128)} %get-tuple-element.418, bf16[2,8,4,4,768]{4,1,3,2,0:T(8,128)(2,1)S(1)} %get-tuple-element.504, f32[2,8,4,4,768]{4,1,3,2,0:T(8,128)S(1)} %multiply_add_fusion.1, f32[768]{0:T(1024)S(1)} %get-tuple-element.471, f32[768]{0:T(1024)S(1)} %get-tuple-element.472, ...), kind=kOutput, calls=%fused_computation.25 | convolution fusion | flops 305332224 | bytes 5913600 | tf_op jit(solution)/shard_map/while/body/eval_jaxpr/cond/branch_1_fun/dot_general | solution.py:131
  127.0 9.0 %collective-permute-done = bf16[2,8,4,4,768]{4,1,3,2,0:T(8,128)(2,1)S(1)} collective-permute-done((bf16[2,8,4,4,768]{4,1,3,2,0:T(8,128)(2,1)S(1)}, bf16[2,8,4,4,768]{4,1,3,2,0:T(8,128)(2,1)S(1)}, u32[]{:S(2)}, u32[]{:S(2)}) %collective-permute-start) | collective-permute-done | bytes 393248 | tf_op jit(solution)/shard_map/while/body/eval_jaxpr/ppermute | solution.py:14
  136.0 14.6 %conditional.2 = (bf16[2,8,4,4,768]{4,1,3,2,0:T(8,128)(2,1)S(1)}, f32[768,768]{1,0:T(8,128)}, f32[9,768]{1,0:T(8,128)}, f32[5,768]{1,0:T(8,128)}) conditional(s32[]{:T(128)} %convert_element_type.67, (f32[768,768]{1,0:T(8,128)}, f32[9,768]{1,0:T(8,128)}, f32[5,768]{1,0:T(8,128)}) %tuple.101, (pred[]{:T(512)}, s32[]{:T(128)}, ...), branch_computations={%region_1.1_spmd, %region_2.16_spmd} | conditional | flops 625999872 | bytes 22551692 | solution.py:188
  138.9 2.1 multiply_reduce_fusion
  146.4 4.1 %bitcast_add_fusion = f32[768,768]{1,0:T(8,128)} fusion(f32[768,768]{1,0:T(8,128)} %get-tuple-element.418, bf16[2,8,4,4,768]{4,1,3,2,0:T(8,128)(2,1)S(1)} %get-tuple-element.504, f32[2,8,4,4,768]{4,1,3,2,0:T(8,128)S(1)} %multiply_add_fusion.1, f32[768]{0:T(1024)S(1)} %get-tuple-element.471, f32[768]{0:T(1024)S(1)} %get-tuple-element.472, ...), kind=kOutput, calls=%fused_computation.25 | convolution fusion | flops 305332224 | bytes 5913600 | tf_op jit(solution)/shard_map/while/body/eval_jaxpr/cond/branch_1_fun/dot_general | solution.py:131
  151.8 8.4 %collective-permute-done = bf16[2,8,4,4,768]{4,1,3,2,0:T(8,128)(2,1)S(1)} collective-permute-done((bf16[2,8,4,4,768]{4,1,3,2,0:T(8,128)(2,1)S(1)}, bf16[2,8,4,4,768]{4,1,3,2,0:T(8,128)(2,1)S(1)}, u32[]{:S(2)}, u32[]{:S(2)}) %collective-permute-start) | collective-permute-done | bytes 393248 | tf_op jit(solution)/shard_map/while/body/eval_jaxpr/ppermute | solution.py:14
  160.2 14.6 %conditional.2 = (bf16[2,8,4,4,768]{4,1,3,2,0:T(8,128)(2,1)S(1)}, f32[768,768]{1,0:T(8,128)}, f32[9,768]{1,0:T(8,128)}, f32[5,768]{1,0:T(8,128)}) conditional(s32[]{:T(128)} %convert_element_type.67, (f32[768,768]{1,0:T(8,128)}, f32[9,768]{1,0:T(8,128)}, f32[5,768]{1,0:T(8,128)}) %tuple.101, (pred[]{:T(512)}, s32[]{:T(128)}, ...), branch_computations={%region_1.1_spmd, %region_2.16_spmd} | conditional | flops 625999872 | bytes 22551692 | solution.py:188
  163.1 2.1 multiply_reduce_fusion
  170.7 4.1 %bitcast_add_fusion = f32[768,768]{1,0:T(8,128)} fusion(f32[768,768]{1,0:T(8,128)} %get-tuple-element.418, bf16[2,8,4,4,768]{4,1,3,2,0:T(8,128)(2,1)S(1)} %get-tuple-element.504, f32[2,8,4,4,768]{4,1,3,2,0:T(8,128)S(1)} %multiply_add_fusion.1, f32[768]{0:T(1024)S(1)} %get-tuple-element.471, f32[768]{0:T(1024)S(1)} %get-tuple-element.472, ...), kind=kOutput, calls=%fused_computation.25 | convolution fusion | flops 305332224 | bytes 5913600 | tf_op jit(solution)/shard_map/while/body/eval_jaxpr/cond/branch_1_fun/dot_general | solution.py:131
  176.0 8.4 %collective-permute-done = bf16[2,8,4,4,768]{4,1,3,2,0:T(8,128)(2,1)S(1)} collective-permute-done((bf16[2,8,4,4,768]{4,1,3,2,0:T(8,128)(2,1)S(1)}, bf16[2,8,4,4,768]{4,1,3,2,0:T(8,128)(2,1)S(1)}, u32[]{:S(2)}, u32[]{:S(2)}) %collective-permute-start) | collective-permute-done | bytes 393248 | tf_op jit(solution)/shard_map/while/body/eval_jaxpr/ppermute | solution.py:14
  184.4 63.0 %all-reduce.4 = (f32[9,768]{1,0:T(8,128)S(1)}, f32[5,768]{1,0:T(8,128)S(1)}) all-reduce(f32[9,768]{1,0:T(8,128)} %get-tuple-element.445, f32[5,768]{1,0:T(8,128)} %get-tuple-element.446), channel_id=1, replica_groups=mesh['dp'=16,'section'=2] {'dp'}, use_global_device_ids=true, to_apply=%region_19.20 | all-reduce | flops 10752 | bytes 86016 | tf_op jit(solution)/shard_map/psum | solution.py:202
  248.7 2.7 %reduce-scatter.2.cloned.1.call-done = f32[48,768]{1,0:T(8,128)} async-done(((f32[768,768]{1,0:T(8,128)}), f32[48,768]{1,0:T(8,128)}) %reduce-scatter.2.cloned.1.call-update) | async-done | bytes 147472 | tf_op jit(solution)/shard_map/reduce_scatter | solution.py:201
  (140 shorter events, 58.4 us)
Async XLA Ops:
  7.2 13.1 %copy-start = (bf16[4,128,768]{2,1,0:T(8,128)(2,1)S(1)}, bf16[4,128,768]{2,1,0:T(8,128)(2,1)}, u32[]{:S(2)}) copy-start(bf16[4,128,768]{2,1,0:T(8,128)(2,1)} %param.17) | copy-start | bytes 2359300
  7.2 244.1 %reduce-scatter.2.cloned.1.call-start = ((), (), s32[]{:S(2)}) async-start(), calls=%async_computation.1 | async-start | bytes 2506752 | tf_op jit(solution)/shard_map/reduce_scatter | solution.py:201
  7.2 1.6 collective-permute-start.1
  9.9 8.7 %collective-permute-start.2 = (bf16[96,768]{1,0:T(8,128)(2,1)S(1)}, bf16[96,768]{1,0:T(8,128)(2,1)S(1)}, u32[]{:S(2)}, u32[]{:S(2)}) collective-permute-start(bf16[96,768]{1,0:T(8,128)(2,1)S(1)} %maximum_select_fusion.3), channel_id=1, source_target_pairs={{0,4},{2,6},{4,0},{6,2},{8,12},{10,14},{12,8},{14,10},{16,20},{18,... | collective-permute-start | bytes 442376 | tf_op jit(solution)/shard_map/ppermute | solution.py:158
  15.5 4.8 %copy-start.3 = (s32[8]{0:T(128)S(1)}, s32[8]{0:T(128)}, u32[]{:S(2)}) copy-start(s32[8]{0:T(128)} %param.13) | copy-start | bytes 100
  18.6 8.9 %collective-permute-start.3 = (bf16[192,768]{1,0:T(8,128)(2,1)S(1)}, bf16[192,768]{1,0:T(8,128)(2,1)S(1)}, u32[]{:S(2)}, u32[]{:S(2)}) collective-permute-start(bf16[192,768]{1,0:T(8,128)(2,1)S(1)} %maximum_select_fusion.2), channel_id=1, source_target_pairs={{0,8},{2,10},{4,12},{6,14},{8,0},{10,2},{12,4},{14,6},{16,24},{18,... | collective-permute-start | bytes 884744 | tf_op jit(solution)/shard_map/ppermute | solution.py:158
  20.3 10.0 %copy-start.2 = (bf16[8,8,4,4,128]{4,3,2,1,0:T(4,128)(2,1)S(1)}, bf16[8,8,4,4,128]{4,3,2,1,0:T(4,128)(2,1)}, u32[]{:S(2)}) copy-start(bf16[8,8,4,4,128]{4,3,2,1,0:T(4,128)(2,1)} %param.12) | copy-start | bytes 786436
  27.7 27.8 %collective-permute-start.4 = (bf16[384,768]{1,0:T(8,128)(2,1)S(1)}, bf16[384,768]{1,0:T(8,128)(2,1)S(1)}, u32[]{:S(2)}, u32[]{:S(2)}) collective-permute-start(bf16[384,768]{1,0:T(8,128)(2,1)S(1)} %maximum_select_fusion.1), channel_id=1, source_target_pairs={{0,16},{2,18},{4,20},{6,22},{8,24},{10,26},{12,28},{14,30},{16,0},... | collective-permute-start | bytes 1769480 | tf_op jit(solution)/shard_map/ppermute | solution.py:158
  59.9 25.5 %collective-permute-start = (bf16[2,8,4,4,768]{4,1,3,2,0:T(8,128)(2,1)S(1)}, bf16[2,8,4,4,768]{4,1,3,2,0:T(8,128)(2,1)S(1)}, u32[]{:S(2)}, u32[]{:S(2)}) collective-permute-start(bf16[2,8,4,4,768]{4,1,3,2,0:T(8,128)(2,1)S(1)} %get-tuple-element.591), channel_id=1, source_target_pairs={{1,0},{3,2},{5,4},{7,6},{9,8},{11,10},{13,12},{15,14},{17,16},{19,... | collective-permute-start | bytes 1179656 | tf_op jit(solution)/shard_map/while/body/eval_jaxpr/ppermute | solution.py:14
  85.4 2.9 %copy-start.1 = (bf16[768,768]{1,0:T(8,128)(2,1)S(1)}, bf16[768,768]{1,0:T(8,128)(2,1)}, u32[]{:S(2)}) copy-start(bf16[768,768]{1,0:T(8,128)(2,1)} %get-tuple-element.416) | copy-start | bytes 3538948 | tf_op jit(solution)/shard_map/while/body/eval_jaxpr/cond
  99.9 11.2 %collective-permute-start = (bf16[2,8,4,4,768]{4,1,3,2,0:T(8,128)(2,1)S(1)}, bf16[2,8,4,4,768]{4,1,3,2,0:T(8,128)(2,1)S(1)}, u32[]{:S(2)}, u32[]{:S(2)}) collective-permute-start(bf16[2,8,4,4,768]{4,1,3,2,0:T(8,128)(2,1)S(1)} %get-tuple-element.591), channel_id=1, source_target_pairs={{1,0},{3,2},{5,4},{7,6},{9,8},{11,10},{13,12},{15,14},{17,16},{19,... | collective-permute-start | bytes 1179656 | tf_op jit(solution)/shard_map/while/body/eval_jaxpr/ppermute | solution.py:14
  111.1 2.9 %copy-start.1 = (bf16[768,768]{1,0:T(8,128)(2,1)S(1)}, bf16[768,768]{1,0:T(8,128)(2,1)}, u32[]{:S(2)}) copy-start(bf16[768,768]{1,0:T(8,128)(2,1)} %get-tuple-element.416) | copy-start | bytes 3538948 | tf_op jit(solution)/shard_map/while/body/eval_jaxpr/cond
  125.7 10.3 %collective-permute-start = (bf16[2,8,4,4,768]{4,1,3,2,0:T(8,128)(2,1)S(1)}, bf16[2,8,4,4,768]{4,1,3,2,0:T(8,128)(2,1)S(1)}, u32[]{:S(2)}, u32[]{:S(2)}) collective-permute-start(bf16[2,8,4,4,768]{4,1,3,2,0:T(8,128)(2,1)S(1)} %get-tuple-element.591), channel_id=1, source_target_pairs={{1,0},{3,2},{5,4},{7,6},{9,8},{11,10},{13,12},{15,14},{17,16},{19,... | collective-permute-start | bytes 1179656 | tf_op jit(solution)/shard_map/while/body/eval_jaxpr/ppermute | solution.py:14
  136.0 2.9 %copy-start.1 = (bf16[768,768]{1,0:T(8,128)(2,1)S(1)}, bf16[768,768]{1,0:T(8,128)(2,1)}, u32[]{:S(2)}) copy-start(bf16[768,768]{1,0:T(8,128)(2,1)} %get-tuple-element.416) | copy-start | bytes 3538948 | tf_op jit(solution)/shard_map/while/body/eval_jaxpr/cond
  150.5 9.7 %collective-permute-start = (bf16[2,8,4,4,768]{4,1,3,2,0:T(8,128)(2,1)S(1)}, bf16[2,8,4,4,768]{4,1,3,2,0:T(8,128)(2,1)S(1)}, u32[]{:S(2)}, u32[]{:S(2)}) collective-permute-start(bf16[2,8,4,4,768]{4,1,3,2,0:T(8,128)(2,1)S(1)} %get-tuple-element.591), channel_id=1, source_target_pairs={{1,0},{3,2},{5,4},{7,6},{9,8},{11,10},{13,12},{15,14},{17,16},{19,... | collective-permute-start | bytes 1179656 | tf_op jit(solution)/shard_map/while/body/eval_jaxpr/ppermute | solution.py:14
  160.2 2.9 %copy-start.1 = (bf16[768,768]{1,0:T(8,128)(2,1)S(1)}, bf16[768,768]{1,0:T(8,128)(2,1)}, u32[]{:S(2)}) copy-start(bf16[768,768]{1,0:T(8,128)(2,1)} %get-tuple-element.416) | copy-start | bytes 3538948 | tf_op jit(solution)/shard_map/while/body/eval_jaxpr/cond
  174.8 9.7 %collective-permute-start = (bf16[2,8,4,4,768]{4,1,3,2,0:T(8,128)(2,1)S(1)}, bf16[2,8,4,4,768]{4,1,3,2,0:T(8,128)(2,1)S(1)}, u32[]{:S(2)}, u32[]{:S(2)}) collective-permute-start(bf16[2,8,4,4,768]{4,1,3,2,0:T(8,128)(2,1)S(1)} %get-tuple-element.591), channel_id=1, source_target_pairs={{1,0},{3,2},{5,4},{7,6},{9,8},{11,10},{13,12},{15,14},{17,16},{19,... | collective-permute-start | bytes 1179656 | tf_op jit(solution)/shard_map/while/body/eval_jaxpr/ppermute | solution.py:14
Sparse Core Ops, SparseCore 0:
  184.6 66.7 reduce-scatter.1
